TPU v7x, 32 devices: a whole 2x2x4 slice. The times are simulated.
32 devices in a mesh: grp: 2 (over core), ep: 16 (over z, y, x).
Axes of the slice: x: 2, y: 2, z: 4, core: 2. Of those that a mesh axis runs over, the one named last changes fastest.
Arguments:
- out_grad: bfloat16 [16384, 2048], P(('grp', 'ep')), may hold values from -0.5 to 0.5
- probs: float32 [16384, 8], P(('grp', 'ep')), may hold values from 0.02 to 0.5
- dest: int32 [16384, 8], P(('grp', 'ep')), may hold values from -1 to 49151, as said below
- replica_owner: int32 [2, 16], P('grp'), may hold values from 0 to 15, as said below
- gate_up: bfloat16 [98304, 1536], P(('grp', 'ep')), may hold values from -6 to 6
Outputs:
- d_down: float32 [16, 768, 2048], P('ep', None, 'grp')
Inputs may be any that keep to these rules, and one draw needn't show every extreme that they name: `dest`: copies of one token name distinct rows; a device's copies to slot buffer (j, s) fill the rows of that buffer's block for the device, which is the device's ep index times 96 onward, from its start without gaps; in every draw some device fills its block of some buffer, all 96 rows, and copies beyond a block are dropped. `replica_owner`: each entry names an expert that has its primary slot on that ep index of the group.
All inputs are finite; a program needn't handle non-finite values.
Results may differ from a plain program's by a relative error of at most 0.005.
Values may be sent and summed in bfloat16 or wider, within the bound.
A program may use at most 128 MiB of HBM per device.

v0:
```python
import jax
import jax.numpy as jnp
from jax import lax
from jax.sharding import PartitionSpec as P


def on_device(out_grad, probs, dest, replica_owner, gate_up):
    n_ep = lax.axis_size("ep")
    tokens = out_grad.shape[0]
    width = out_grad.shape[1]
    top = probs.shape[1]
    cap = gate_up.shape[0] // 2
    hidden = gate_up.shape[1] // 2
    per_src = cap // n_ep
    flat = dest.reshape(-1)
    device_of = flat // (2 * cap)
    within = flat % (2 * cap)
    slot_lookup = within // cap
    place = within % per_src
    target = device_of * 2 * per_src + slot_lookup * per_src + place
    target = jnp.where(flat >= 0, target, 2 * cap)
    copy_of = (
        jnp.full((2 * cap,), -1, jnp.int32)
        .at[target]
        .set(jnp.arange(tokens * top, dtype=jnp.int32), mode="drop")
    )
    safe = jnp.maximum(copy_of, 0)
    weight = jnp.where(copy_of >= 0, probs.reshape(-1)[safe], 0.0)
    outgoing = (weight[:, None] * out_grad[safe // top].astype(jnp.float32)).astype(jnp.bfloat16)
    outgoing = outgoing.reshape(n_ep, 2, per_src, width)
    incoming = lax.all_to_all(outgoing, "ep", split_axis=0, concat_axis=2, tiled=True)
    grads = incoming.reshape(2, cap, width)
    act = jax.nn.silu(gate_up[:, :hidden].astype(jnp.float32)) * gate_up[:, hidden:].astype(
        jnp.float32
    )
    act = act.astype(jnp.bfloat16).reshape(2, cap, hidden)
    tiles = jnp.einsum("sch,scd->shd", act, grads, preferred_element_type=jnp.float32).astype(
        jnp.bfloat16
    )
    owners = replica_owner[0]
    experts = jnp.arange(n_ep, dtype=jnp.int32)
    received = lax.all_to_all(tiles[1], "ep", split_axis=0, concat_axis=0, tiled=True)
    pieces = received.reshape(n_ep, -1)
    primary = tiles[0].astype(jnp.float32)
    select = (owners[None, :] == experts[:, None]).astype(jnp.bfloat16)
    block_sums = jnp.dot(select, pieces, preferred_element_type=jnp.float32).reshape(-1, width)
    owned = lax.all_to_all(block_sums, "ep", split_axis=0, concat_axis=0, tiled=True)
    owned = owned + primary
    result = lax.psum_scatter(owned, "grp", scatter_dimension=1, tiled=True)
    return result[None]


def solution(mesh):
    in_specs = (
        P(("grp", "ep"), None),
        P(("grp", "ep"), None),
        P(("grp", "ep"), None),
        P("grp", None),
        P(("grp", "ep"), None),
    )
    out_specs = P("ep", None, "grp")
    return jax.shard_map(
        on_device, mesh=mesh, in_specs=in_specs, out_specs=out_specs, check_vma=False
    )
```

profile of v0, /device:TPU:0, one launch (start us, length us, event | category | flops | bytes accessed | tf_op | source)
XLA Modules:
  0.0 633.6 jit_solution(17132969857570626571)
XLA Ops:
  6.5 0.9 broadcast_divide_fusion
  7.4 0.7 sign_compare_fusion
  8.3 0.2 div.41
  8.6 0.2 rem.59
  8.9 0.2 ge.17
  9.3 0.2 ne.104
  9.5 0.2 compare_select_fusion
  9.7 15.5 %scatter_custom_fusion = s32[3072]{0:T(1024)S(1)} fusion(s32[4096]{0:T(1024)S(1)} %bitcast.41, s32[4096]{0:T(1024)S(1)} %iota.7, s32[]{:T(128)} %constant.55.clone.1), kind=kCustom, calls=%fused_computation.39 | custom fusion | bytes 12292 | tf_op jit(solution)/shard_map/scatter | solution.py:25
  25.3 0.8 copy.23
  26.3 17.4 %gather_fusion = f32[3072]{0:T(1024)S(1)} fusion(f32[4096]{0:T(1024)S(1)} %reshape.175, s32[3072]{0:T(1024)S(1)} %get-tuple-element.9), kind=kCustom, calls=%fused_computation | custom fusion | bytes 36864 | tf_op jit(solution)/shard_map/gather | solution.py:28
  43.8 16.0 %gather_fusion.1 = bf16[3072,2048]{1,0:T(8,128)(2,1)} fusion(bf16[512,2048]{1,0:T(8,128)(2,1)S(1)} %copy-done, s32[3072]{0:T(1024)S(1)} %get-tuple-element.10), kind=kCustom, calls=%fused_computation.1 | custom fusion | bytes 25178112 | tf_op jit(solution)/shard_map/gather | solution.py:29
  59.8 11.1 %fusion = bf16[16,2,96,2048]{3,2,1,0:T(8,128)(2,1)} fusion(bf16[16,2,96,2048]{3,2,1,0:T(8,128)(2,1)} %bitcast.34, f32[16,2,96]{2,1,0:T(2,128)S(1)} %mul.47), kind=kLoop, calls=%fused_computation.4 | loop fusion | flops 18874368 | bytes 25178112 | tf_op jit(solution)/shard_map/convert_element_type | solution.py:29
  70.9 8.4 %all-to-all-start = ((bf16[16,2,96,2048]{3,2,1,0:T(8,128)(2,1)}), bf16[16,2,96,2048]{3,2,1,0:T(8,128)(2,1)}, u32[]{:S(2)}, u32[]{:S(2)}) async-start(bf16[16,2,96,2048]{3,2,1,0:T(8,128)(2,1)} %fusion), calls=%async_computation | async-start | bytes 25165824 | tf_op jit(solution)/shard_map/all_to_all | solution.py:31
  79.4 8.0 %fusion.5 = bf16[3072,768]{1,0:T(8,128)(2,1)} fusion(bf16[3072,1536]{1,0:T(8,128)(2,1)} %param.9), kind=kLoop, calls=%fused_computation.11 | loop fusion | flops 18874368 | bytes 14155776 | tf_op jit(solution)/shard_map/convert_element_type | solution.py:36
  87.4 229.1 %all-to-all-done = bf16[16,2,96,2048]{3,2,1,0:T(8,128)(2,1)} async-done(((bf16[16,2,96,2048]{3,2,1,0:T(8,128)(2,1)}), bf16[16,2,96,2048]{3,2,1,0:T(8,128)(2,1)}, u32[]{:S(2)}, u32[]{:S(2)}) %all-to-all-start) | async-done | bytes 12582944 | tf_op jit(solution)/shard_map/all_to_all | solution.py:31
  316.5 6.5 %copy.24 = bf16[1,2,16,96,2048]{4,3,2,1,0:T(8,128)(2,1)S(1)} copy(bf16[1,2,16,96,2048]{4,3,1,2,0:T(8,128)(2,1)} %bitcast.6) | data formatting | bytes 25165824 | tf_op jit(solution)/shard_map/all_to_all | solution.py:31
  323.0 12.0 %convolution_convert_fusion = bf16[2,768,2048]{2,1,0:T(8,128)(2,1)} fusion(bf16[2,1536,768]{2,1,0:T(8,128)(2,1)S(1)} %bitcast.40, bf16[2,1536,2048]{2,1,0:T(8,128)(2,1)S(1)} %bitcast.35), kind=kOutput, calls=%fused_computation.13 | convolution fusion | flops 9666822144 | bytes 23592960 | tf_op jit(solution)/shard_map/sch,scd->shd/dot_general | solution.py:37
  335.0 1.9 slice-done.2
  336.9 124.8 %all_to_all.33 = bf16[16,48,2048]{2,1,0:T(8,128)(2,1)S(1)} all-to-all(bf16[16,48,2048]{2,1,0:T(8,128)(2,1)S(1)} %bitcast.38), channel_id=1, replica_groups=mesh['grp'=2,'ep'=16] {'ep'}, dimensions={0} | all-to-all | bytes 6291456 | tf_op jit(solution)/shard_map/all_to_all | solution.py:42
  461.7 3.6 fusion.6
  465.3 3.6 copy.27
  468.9 141.8 %all_to_all.34 = f32[16,48,2048]{2,1,0:T(8,128)S(1)} all-to-all(f32[16,48,2048]{2,1,0:T(8,128)S(1)} %copy.27), channel_id=1, replica_groups=mesh['grp'=2,'ep'=16] {'ep'}, dimensions={0} | all-to-all | bytes 12582912 | tf_op jit(solution)/shard_map/all_to_all | solution.py:47
  610.8 3.7 convert_add_fusion
  614.5 12.3 %reduce-scatter.2.cloned.1.call-done = f32[768,1024]{1,0:T(8,128)} async-done(((f32[768,2048]{1,0:T(8,128)}), f32[768,1024]{1,0:T(8,128)}) %reduce-scatter.2.cloned.1.call-update) | async-done | bytes 3145744 | tf_op jit(solution)/shard_map/reduce_scatter | solution.py:49
  (25 shorter events, 0.9 us)
Async XLA Ops:
  6.5 37.3 %copy-start = (bf16[512,2048]{1,0:T(8,128)(2,1)S(1)}, bf16[512,2048]{1,0:T(8,128)(2,1)}, u32[]{:S(2)}) copy-start(bf16[512,2048]{1,0:T(8,128)(2,1)} %param.5) | copy-start | bytes 6291460
  70.9 245.6 %all-to-all-start = ((bf16[16,2,96,2048]{3,2,1,0:T(8,128)(2,1)}), bf16[16,2,96,2048]{3,2,1,0:T(8,128)(2,1)}, u32[]{:S(2)}, u32[]{:S(2)}) async-start(bf16[16,2,96,2048]{3,2,1,0:T(8,128)(2,1)} %fusion), calls=%async_computation | async-start | bytes 25165824 | tf_op jit(solution)/shard_map/all_to_all | solution.py:31
  79.3 547.4 %reduce-scatter.2.cloned.1.call-start = ((), (), s32[]{:S(2)}) async-start(), calls=%async_computation.4 | async-start | bytes 9437184 | tf_op jit(solution)/shard_map/reduce_scatter | solution.py:49
  316.5 6.5 %copy-start.2 = (bf16[3072,768]{1,0:T(8,128)(2,1)S(1)}, bf16[3072,768]{1,0:T(8,128)(2,1)}, u32[]{:S(2)}) copy-start(bf16[3072,768]{1,0:T(8,128)(2,1)} %fusion.5) | copy-start | bytes 14155780
  335.0 1.9 slice-start.2
  335.0 126.7 %copy-start.3 = (s32[1,16]{1,0:T(1,128)S(1)}, s32[1,16]{1,0:T(1,128)}, u32[]{:S(2)}) copy-start(s32[1,16]{1,0:T(1,128)} %param.8) | copy-start | bytes 196
  465.3 145.5 %slice-start = ((s8[6291456]{0:T(1024)(128)(4,1)}), s8[4194304]{0:T(1024)(128)(4,1)S(1)}, s32[]{:S(2)}) async-start(s8[6291456]{0:T(1024)(128)(4,1)} %bitcast.36), calls=%async_computation.5 | async-start | bytes 8388608
  468.9 141.8 %slice-start.1 = ((s8[6291456]{0:T(1024)(128)(4,1)}), s8[2097152]{0:T(1024)(128)(4,1)S(1)}, s32[]{:S(2)}) async-start(s8[6291456]{0:T(1024)(128)(4,1)} %bitcast.36), calls=%async_computation.6 | async-start | bytes 4194304
  610.7 16.0 %copy-start.1 = (bf16[512,2048]{1,0:T(8,128)(2,1)S(1)}, bf16[512,2048]{1,0:T(8,128)(2,1)}, u32[]{:S(2)}) copy-start(bf16[512,2048]{1,0:T(8,128)(2,1)} %param.5) | copy-start | bytes 6291460
Sparse Core Ops, SparseCore 0:
  614.6 12.1 reduce-scatter.1
where the time goes:
time: 634 us
  blocking collectives  267 us (42%)
  waiting for transfers between devices  241 us (38%)
  local copies, waits for them, and re-layouts  63.3 us (10%)
  other arithmetic  24.7 us (4%)
  matrix products  15.6 us (2%)
  between operations  13.6 us (2%)
  starting transfers between devices  8.43 us (1%)
    all_to_all x1, waiting for transfers between devices, on_device(): lax.all_to_all(outgoing, 'ep', split_axis=0, concat_axis=2, tiled=True)  229 us
    all_to_all x1, blocking collectives, on_device(): lax.all_to_all(block_sums, 'ep', split_axis=0, concat_axis=0, tiled=True)  142 us
    all_to_all x1, blocking collectives, on_device(): lax.all_to_all(tiles[1], 'ep', split_axis=0, concat_axis=0, tiled=True)  125 us
    gather x1, local copies, waits for them, and re-layouts, on_device(): weight = jnp.where(copy_of >= 0, probs.reshape(-1)[safe], 0.0)  17.4 us
    gather x1, local copies, waits for them, and re-layouts, on_device(): out_grad[safe // top].astype(jnp.float32)  16 us
    scatter x1, local copies, waits for them, and re-layouts, on_device(): copy_of = jnp.full((2 * cap,), -1, jnp.int32).at[target].set(jnp.arange(t...  15.5 us
  transfers between devices with their start and end apart: 2, of which 2 were waited for; matrix products, arithmetic and copies ran while one was open for 1% of the time, Pallas kernels for 0%

commit v1 on v0

--- a/solution.py
+++ b/solution.py
@@ -28,7 +28,13 @@
     weight = jnp.where(copy_of >= 0, probs.reshape(-1)[safe], 0.0)
     outgoing = (weight[:, None] * out_grad[safe // top].astype(jnp.float32)).astype(jnp.bfloat16)
     outgoing = outgoing.reshape(n_ep, 2, per_src, width)
-    incoming = lax.all_to_all(outgoing, "ep", split_axis=0, concat_axis=2, tiled=True)
+
+    def modes_report(page, array_dim, dim_i=2):
+        v_now = jnp.split(page, lax.psum(1, axis_name="ep"), axis=array_dim)
+        b_next = lax.all_to_all(jnp.stack(v_now), axis_name="ep", split_axis=0, concat_axis=0)
+        return jnp.concatenate(b_next, axis=dim_i)
+
+    incoming = modes_report(outgoing, 0)
     grads = incoming.reshape(2, cap, width)
     act = jax.nn.silu(gate_up[:, :hidden].astype(jnp.float32)) * gate_up[:, hidden:].astype(
         jnp.float32

time: 634 us -> 649 us (1.024)
  local copies, waits for them, and re-layouts: 63.3 us -> 81.5 us
    unnamed x13 -> x28, local copies, waits for them, and re-layouts: 0.86 us -> 15.5 us
where the time goes in v1:
time: 649 us; the launch traced here: 648 us
  blocking collectives  267 us (41%)
  waiting for transfers between devices  241 us (37%)
  local copies, waits for them, and re-layouts  81.5 us (13%)
  other arithmetic  20.8 us (3%)
  matrix products  15.6 us (2%)
  between operations  13.6 us (2%)
  starting transfers between devices  8.43 us (1%)
    all_to_all x1, waiting for transfers between devices, modes_report(): lax.all_to_all(jnp.stack(v_now), axis_name='ep', split_axis=0, concat_axi...  229 us
    all_to_all x1, blocking collectives, on_device(): lax.all_to_all(block_sums, 'ep', split_axis=0, concat_axis=0, tiled=True)  142 us
    all_to_all x1, blocking collectives, on_device(): lax.all_to_all(tiles[1], 'ep', split_axis=0, concat_axis=0, tiled=True)  125 us
    gather x1, local copies, waits for them, and re-layouts, on_device(): weight = jnp.where(copy_of >= 0, probs.reshape(-1)[safe], 0.0)  17.4 us
    gather x1, local copies, waits for them, and re-layouts, on_device(): out_grad[safe // top].astype(jnp.float32)  16 us
    scatter x1, local copies, waits for them, and re-layouts, on_device(): copy_of = jnp.full((2 * cap,), -1, jnp.int32).at[target].set(jnp.arange(t...  15.5 us
    unnamed x28, local copies, waits for them, and re-layouts  15.5 us
  transfers between devices with their start and end apart: 2, of which 2 were waited for; matrix products, arithmetic and copies ran while one was open for 1% of the time, Pallas kernels for 0%

profile of v1, /device:TPU:0, one launch (start us, length us, event | category | flops | bytes accessed | tf_op | source)
XLA Modules:
  0.0 648.1 jit_solution(3947122857836698353)
XLA Ops:
  9.7 15.5 %scatter_custom_fusion = s32[3072]{0:T(1024)S(1)} fusion(s32[4096]{0:T(1024)S(1)} %bitcast.68, s32[4096]{0:T(1024)S(1)} %iota.7, s32[]{:T(128)} %constant.55.clone.1), kind=kCustom, calls=%fused_computation.54 | custom fusion | bytes 12292 | tf_op jit(solution)/shard_map/scatter | solution.py:25
  26.3 17.4 %gather_fusion = f32[3072]{0:T(1024)S(1)} fusion(f32[4096]{0:T(1024)S(1)} %reshape.198, s32[3072]{0:T(1024)S(1)} %get-tuple-element.25), kind=kCustom, calls=%fused_computation | custom fusion | bytes 36864 | tf_op jit(solution)/shard_map/gather | solution.py:28
  43.7 16.0 %gather_fusion.1 = bf16[3072,2048]{1,0:T(8,128)(2,1)} fusion(bf16[512,2048]{1,0:T(8,128)(2,1)S(1)} %copy-done, s32[3072]{0:T(1024)S(1)} %get-tuple-element.26), kind=kCustom, calls=%fused_computation.1 | custom fusion | bytes 25178112 | tf_op jit(solution)/shard_map/gather | solution.py:29
  59.7 7.2 %multiply_convert_fusion = bf16[3072,2048]{1,0:T(8,128)(2,1)S(1)} fusion(bf16[3072,2048]{1,0:T(8,128)(2,1)} %gather_fusion.1, f32[3072]{0:T(1024)S(1)} %compare_select_fusion.2), kind=kLoop, calls=%fused_computation.3 | loop fusion | flops 18874368 | bytes 25178112 | tf_op jit(solution)/shard_map/convert_element_type | solution.py:29
  66.9 2.2 fusion.17
  69.2 1.0 constant_dynamic-update-slice_fusion.15
  72.2 1.0 constant_dynamic-update-slice_fusion.12
  73.1 1.0 constant_dynamic-update-slice_fusion.11
  75.1 1.0 constant_dynamic-update-slice_fusion.9
  78.0 1.0 constant_dynamic-update-slice_fusion.6
  80.9 1.0 constant_dynamic-update-slice_fusion.3
  83.9 1.0 constant_dynamic-update-slice_fusion
  84.9 8.4 %all-to-all-start = ((bf16[16,1,2,96,2048]{4,3,2,1,0:T(8,128)(2,1)}), bf16[16,1,2,96,2048]{4,3,2,1,0:T(8,128)(2,1)}, u32[]{:S(2)}, u32[]{:S(2)}) async-start(bf16[16,1,2,96,2048]{4,3,2,1,0:T(8,128)(2,1)} %constant_dynamic-update-slice_fusion), calls=%async_computation | async-start | bytes 25165824 | tf_op jit(solution)/shard_map/all_to_all | solution.py:34
  93.3 8.0 %fusion.4 = bf16[3072,768]{1,0:T(8,128)(2,1)} fusion(bf16[3072,1536]{1,0:T(8,128)(2,1)} %param.9), kind=kLoop, calls=%fused_computation.10 | loop fusion | flops 18874368 | bytes 14155776 | tf_op jit(solution)/shard_map/convert_element_type | solution.py:42
  101.3 229.1 %all-to-all-done = bf16[16,1,2,96,2048]{4,3,2,1,0:T(8,128)(2,1)} async-done(((bf16[16,1,2,96,2048]{4,3,2,1,0:T(8,128)(2,1)}), bf16[16,1,2,96,2048]{4,3,2,1,0:T(8,128)(2,1)}, u32[]{:S(2)}, u32[]{:S(2)}) %all-to-all-start) | async-done | bytes 12582944 | tf_op jit(solution)/shard_map/all_to_all | solution.py:34
  330.5 6.5 copy.53
  337.0 12.0 %convolution_convert_fusion = bf16[2,768,2048]{2,1,0:T(8,128)(2,1)} fusion(bf16[2,1536,768]{2,1,0:T(8,128)(2,1)S(1)} %bitcast.51, bf16[2,1536,2048]{2,1,0:T(8,128)(2,1)S(1)} %bitcast.46), kind=kOutput, calls=%fused_computation.12 | convolution fusion | flops 9666822144 | bytes 23592960 | tf_op jit(solution)/shard_map/sch,scd->shd/dot_general | solution.py:43
  348.9 2.3 slice.36
  351.3 124.8 %all_to_all.23 = bf16[16,48,2048]{2,1,0:T(8,128)(2,1)S(1)} all-to-all(bf16[16,48,2048]{2,1,0:T(8,128)(2,1)S(1)} %bitcast.47), channel_id=1, replica_groups=mesh['grp'=2,'ep'=16] {'ep'}, dimensions={0} | all-to-all | bytes 6291456 | tf_op jit(solution)/shard_map/all_to_all | solution.py:48
  476.1 3.6 fusion.5
  479.6 3.6 copy.56
  483.3 141.9 %all_to_all.24 = f32[16,48,2048]{2,1,0:T(8,128)S(1)} all-to-all(f32[16,48,2048]{2,1,0:T(8,128)S(1)} %copy.56), channel_id=1, replica_groups=mesh['grp'=2,'ep'=16] {'ep'}, dimensions={0} | all-to-all | bytes 12582912 | tf_op jit(solution)/shard_map/all_to_all | solution.py:53
  625.2 3.7 convert_add_fusion
  629.0 12.3 %reduce-scatter.2.cloned.1.call-done = f32[768,1024]{1,0:T(8,128)} async-done(((f32[768,2048]{1,0:T(8,128)}), f32[768,1024]{1,0:T(8,128)}) %reduce-scatter.2.cloned.1.call-update) | async-done | bytes 3145744 | tf_op jit(solution)/shard_map/reduce_scatter | solution.py:55
  (40 shorter events, 12.9 us)
Async XLA Ops:
  6.5 37.2 %copy-start = (bf16[512,2048]{1,0:T(8,128)(2,1)S(1)}, bf16[512,2048]{1,0:T(8,128)(2,1)}, u32[]{:S(2)}) copy-start(bf16[512,2048]{1,0:T(8,128)(2,1)} %param.5) | copy-start | bytes 6291460
  84.9 245.6 %all-to-all-start = ((bf16[16,1,2,96,2048]{4,3,2,1,0:T(8,128)(2,1)}), bf16[16,1,2,96,2048]{4,3,2,1,0:T(8,128)(2,1)}, u32[]{:S(2)}, u32[]{:S(2)}) async-start(bf16[16,1,2,96,2048]{4,3,2,1,0:T(8,128)(2,1)} %constant_dynamic-update-slice_fusion), calls=%async_computation | async-start | bytes 25165824 | tf_op jit(solution)/shard_map/all_to_all | solution.py:34
  93.3 548.0 %reduce-scatter.2.cloned.1.call-start = ((), (), s32[]{:S(2)}) async-start(), calls=%async_computation.4 | async-start | bytes 9437184 | tf_op jit(solution)/shard_map/reduce_scatter | solution.py:55
  330.5 6.5 copy-start.2
  348.9 127.1 %copy-start.3 = (s32[1,16]{1,0:T(1,128)S(1)}, s32[1,16]{1,0:T(1,128)}, u32[]{:S(2)}) copy-start(s32[1,16]{1,0:T(1,128)} %param.8) | copy-start | bytes 196
  479.6 145.6 %slice-start = ((s8[6291456]{0:T(1024)(128)(4,1)}), s8[4194304]{0:T(1024)(128)(4,1)S(1)}, s32[]{:S(2)}) async-start(s8[6291456]{0:T(1024)(128)(4,1)} %bitcast.49), calls=%async_computation.5 | async-start | bytes 8388608
  483.3 142.0 %slice-start.1 = ((s8[6291456]{0:T(1024)(128)(4,1)}), s8[2097152]{0:T(1024)(128)(4,1)S(1)}, s32[]{:S(2)}) async-start(s8[6291456]{0:T(1024)(128)(4,1)} %bitcast.49), calls=%async_computation.6 | async-start | bytes 4194304
  483.3 157.9 %copy-start.1 = (bf16[512,2048]{1,0:T(8,128)(2,1)S(1)}, bf16[512,2048]{1,0:T(8,128)(2,1)}, u32[]{:S(2)}) copy-start(bf16[512,2048]{1,0:T(8,128)(2,1)} %param.5) | copy-start | bytes 6291460
Sparse Core Ops, SparseCore 0:
  629.1 12.1 reduce-scatter.1
